TPU v7x, 512 devices: a whole 4x8x8 slice. The times are simulated.
512 devices in a mesh: tm: 256 (over z, y, x), space: 2 (over core).
Axes of the slice: x: 4, y: 8, z: 8, core: 2. Of those that a mesh axis runs over, the one named last changes fastest.
Arguments:
- image_gradient: bfloat16 [512, 128, 3, 4096], P('tm', 'space'), may hold values from -0.375 to 0.375
- residual: bfloat16 [512, 128, 4096], P('tm', 'space'), may hold values from -6 to 6
- phase: float32 [512], P('tm'), may hold values from 0 to 1
- counts: int32 [128], P('space'), may hold values from 512 to 4096
- owner: int32 [128, 1], P('space'), may hold values from 0 to 1, as said below
Outputs:
- hessian_blocks: float32 [512, 192, 576], P('tm', 'space')
- gradient_blocks: float32 [512, 192, 24], P('tm', 'space')
Inputs may be any that keep to these rules, and one draw needn't show every extreme that they name: Among the 64 bricks of each aligned block at most 48 share an owner, and one owner takes exactly 48 bricks of every block.
All inputs are finite; a program needn't handle non-finite values.
Results may differ from a plain program's by a relative error of at most 0.0029.
Values sent between devices are 32-bit elements; how exact they have to be, the bound alone decides.
A program may use at most 64 MiB of HBM per device.

v0:
```python
import jax
import jax.numpy as jnp
from jax import lax
from jax.sharding import PartitionSpec as P

EDGE = 16


def shifted(block, axis, distance):
    devices = range(lax.axis_size(axis))
    route = [(i - distance, i) for i in devices if i - distance in devices]
    return lax.ppermute(block, axis, route)


def spline_weights(phase):
    return jnp.stack(
        [
            (1.0 - phase) ** 3 / 6.0,
            (3.0 * phase**3 - 6.0 * phase**2 + 4.0) / 6.0,
            (-3.0 * phase**3 + 3.0 * phase**2 + 3.0 * phase + 1.0) / 6.0,
            phase**3 / 6.0,
        ],
        axis=-1,
    )


def shape_table(edge):
    voxel = jnp.arange(edge * edge * edge, dtype=jnp.int32)
    first = ((voxel // (edge * edge)).astype(jnp.float32) + 0.5) / edge
    second = ((voxel // edge % edge).astype(jnp.float32) + 0.5) / edge
    third = ((voxel % edge).astype(jnp.float32) + 0.5) / edge
    rows = []
    for node in range(8):
        along_first = first if node >> 2 & 1 else 1.0 - first
        along_second = second if node >> 1 & 1 else 1.0 - second
        along_third = third if node & 1 else 1.0 - third
        rows.append(along_first * along_second * along_third)
    return jnp.stack(rows, axis=0)


def per_device(image_gradient, residual, phase, counts, owner):
    step_count, brick_count, comp_count, voxel_count = image_gradient.shape
    dof_count = 8 * comp_count
    patch_width = dof_count * dof_count
    column_count = patch_width + dof_count
    first_step = lax.axis_index("tm") * step_count
    overall_step_count = lax.axis_size("tm") * step_count
    space_count = lax.axis_size("space")
    capacity = 3 * brick_count // (2 * space_count)
    valid_mask = lax.broadcasted_iota(jnp.int32, (brick_count, voxel_count), 1) < counts[:, None]
    shapes = shape_table(EDGE)

    def per_step(pair):
        grads, resid = pair
        product = shapes[None, :, None, :] * grads.astype(jnp.float32)[:, None, :, :]
        sens = product.reshape(brick_count, dof_count, voxel_count).astype(jnp.bfloat16)
        masked = jnp.where(valid_mask[:, None, :], sens, jnp.zeros((), jnp.bfloat16))
        hessian = jnp.einsum("bdv,bev->bde", masked, masked, preferred_element_type=jnp.float32)
        gradient = jnp.einsum("bdv,bv->bd", masked, resid, preferred_element_type=jnp.float32)
        return jnp.concatenate([hessian.reshape(brick_count, patch_width), gradient], axis=1)

    patch_contents = lax.map(per_step, (image_gradient, residual))
    weights = spline_weights(phase)
    global_step = first_step + jnp.arange(step_count, dtype=jnp.int32)
    target = jnp.clip(
        global_step[:, None] - 1 + jnp.arange(4, dtype=jnp.int32)[None, :],
        0,
        overall_step_count - 1,
    )
    local_slot = target - first_step + 1
    hits_table = (
        local_slot[:, :, None] == jnp.arange(step_count + 3, dtype=jnp.int32)[None, None, :]
    ).astype(jnp.float32)
    basis_lookup_grid = jnp.sum(weights[:, :, None] * hits_table, axis=1)
    is_hessian_column = (jnp.arange(column_count, dtype=jnp.int32) < patch_width)[None, None, :]
    multiplier = jnp.where(
        is_hessian_column,
        (basis_lookup_grid * basis_lookup_grid)[:, :, None],
        basis_lookup_grid[:, :, None],
    )
    owner_flat = owner[:, 0]
    owner_hits = (owner_flat[:, None] == jnp.arange(space_count, dtype=jnp.int32)[None, :]).astype(
        jnp.int32
    )
    earlier = jnp.cumsum(owner_hits, axis=0) - owner_hits
    brick_rank = jnp.sum(earlier * owner_hits, axis=1)
    destination = owner_flat * capacity + brick_rank
    slot_match = (
        destination[:, None] == jnp.arange(space_count * capacity, dtype=jnp.int32)[None, :]
    )
    source_brick = jnp.sum(
        jnp.where(slot_match, jnp.arange(brick_count, dtype=jnp.int32)[:, None], 0), axis=0
    )
    slot_filled = jnp.any(slot_match, axis=0)
    packed = multiplier[0][:, None, :] * patch_contents[0][None]
    packed = packed + multiplier[1][:, None, :] * patch_contents[1][None]
    from_before = shifted(packed[step_count + 1 :], "tm", 1)
    behind = shifted(packed[:1], "tm", -1)
    own_part = packed[1 : step_count + 1]
    own_part = own_part.at[:2].add(from_before)
    picked = jnp.take(own_part.at[step_count - 1 :].add(behind), source_brick, axis=1)
    placed = jnp.where(slot_filled[None, :, None], picked, jnp.zeros((), jnp.float32))
    result = lax.all_to_all(placed, "space", split_axis=1, concat_axis=1, tiled=True)
    return (result[:, :, :patch_width], result[:, :, patch_width:])


def solution(mesh):
    in_specs = (
        P("tm", "space", None, None),
        P("tm", "space", None),
        P("tm"),
        P("space"),
        P("space", None),
    )
    out_specs = (P("tm", "space", None), P("tm", "space", None))
    return jax.shard_map(
        per_device, mesh=mesh, in_specs=in_specs, out_specs=out_specs, check_vma=False
    )
```

profile of v0, /device:TPU:255, one launch (start us, length us, event | category | flops | bytes accessed | tf_op | source)
XLA Modules:
  0.0 134.0 jit_solution(4634049659191790835)
XLA Ops:
  0.6 0.1 fusion.30
  0.7 0.1 fusion.24
  0.8 0.1 fusion.28
  0.9 0.1 fusion.22
  1.1 0.2 stack.31
  1.3 102.2 %while.14 = (s32[]{:T(128)}, f32[2,64,600]{1,2,0:T(8,128)}, f32[8,4096]{1,0:T(8,128)S(1)}, bf16[2,64,3,4096]{3,1,2,0:T(8,128)(2,1)}, bf16[2,64,4096]{2,1,0:T(8,128)(2,1)}, /*index=5*/s32[64]{0:T(128)}, s32[]{:T(128)}) while((s32[]{:T(128)}, f32[2,64,600]{1,2,0:T(8,128)}, f32[8,4096]{1,0:T(8,128)S(1)}, ...), condition=%wide.region_6.7_spmd.clone, body=%wide.region_5.6_spmd.clone.sunk | while | flops 334534144 | bytes 58191368 | solution.py:62
  1.3 1.8 %bitcast_convert_fusion.2 = f32[64,3,4096]{2,0,1:T(8,128)S(1)} fusion(bf16[2,64,3,4096]{3,1,2,0:T(8,128)(2,1)} %get-tuple-element.176, s32[]{:T(128)S(6)} %copy.47), kind=kLoop, calls=%fused_computation.9.clone.1 | loop fusion | flops 786432 | bytes 4718596 | tf_op jit(solution)/shard_map/while/body/eval_jaxpr/convert_element_type | solution.py:55
  3.1 0.9 mul.344
  4.0 1.2 mul.345
  5.3 0.2 iota_compare_fusion.6
  5.5 6.0 %fusion.46 = bf16[64,24,4096]{2,0,1:T(8,128)(2,1)} fusion(f32[64,3,4096]{2,0,1:T(8,128)S(1)} %bitcast_convert_fusion.2, f32[24,4096]{1,0:T(8,128)S(1)} %mul.345, pred[64,4096]{1,0:T(8,128)(4,1)S(1)} %iota_compare_fusion.6), kind=kLoop, calls=%fused_computation.4.clone.1 | loop fusion | flops 18874368 | bytes 16384000 | tf_op jit(solution)/shard_map/while/body/eval_jaxpr/jit(_where)/select_n | solution.py:57
  11.6 13.3 %fusion.47 = f32[64,1,24]{2,1,0:T(1,128)S(1)} fusion(bf16[64,24,4096]{2,0,1:T(8,128)(2,1)} %fusion.46, bf16[64,4096,1]{1,0,2:T(8,128)(2,1)S(1)} %dynamic-slice_bitcast_fusion.2), kind=kOutput, calls=%fused_computation.5.clone.1 | convolution fusion | flops 12582912 | bytes 13113344 | tf_op jit(solution)/shard_map/while/body/eval_jaxpr/bdv,bv->bd/dot_general | solution.py:59
  25.0 26.2 %fusion.48 = f32[64,24,24]{2,1,0:T(8,128)S(1)} fusion(bf16[64,24,4096]{2,0,1:T(8,128)(2,1)} %fusion.46), kind=kOutput, calls=%fused_computation.7.clone.1 | convolution fusion | flops 301989888 | bytes 12730368 | tf_op jit(solution)/shard_map/while/body/eval_jaxpr/bdv,bev->bde/dot_general | solution.py:58
  51.2 0.3 copy.43
  51.6 0.8 copy-done.4
  52.4 1.8 %bitcast_convert_fusion.2 = f32[64,3,4096]{2,0,1:T(8,128)S(1)} fusion(bf16[2,64,3,4096]{3,1,2,0:T(8,128)(2,1)} %get-tuple-element.176, s32[]{:T(128)S(6)} %copy.47), kind=kLoop, calls=%fused_computation.9.clone.1 | loop fusion | flops 786432 | bytes 4718596 | tf_op jit(solution)/shard_map/while/body/eval_jaxpr/convert_element_type | solution.py:55
  54.2 0.9 mul.344
  55.1 1.2 mul.345
  56.4 0.2 iota_compare_fusion.6
  56.6 6.0 %fusion.46 = bf16[64,24,4096]{2,0,1:T(8,128)(2,1)} fusion(f32[64,3,4096]{2,0,1:T(8,128)S(1)} %bitcast_convert_fusion.2, f32[24,4096]{1,0:T(8,128)S(1)} %mul.345, pred[64,4096]{1,0:T(8,128)(4,1)S(1)} %iota_compare_fusion.6), kind=kLoop, calls=%fused_computation.4.clone.1 | loop fusion | flops 18874368 | bytes 16384000 | tf_op jit(solution)/shard_map/while/body/eval_jaxpr/jit(_where)/select_n | solution.py:57
  62.7 13.3 %fusion.47 = f32[64,1,24]{2,1,0:T(1,128)S(1)} fusion(bf16[64,24,4096]{2,0,1:T(8,128)(2,1)} %fusion.46, bf16[64,4096,1]{1,0,2:T(8,128)(2,1)S(1)} %dynamic-slice_bitcast_fusion.2), kind=kOutput, calls=%fused_computation.5.clone.1 | convolution fusion | flops 12582912 | bytes 13113344 | tf_op jit(solution)/shard_map/while/body/eval_jaxpr/bdv,bv->bd/dot_general | solution.py:59
  76.1 26.2 %fusion.48 = f32[64,24,24]{2,1,0:T(8,128)S(1)} fusion(bf16[64,24,4096]{2,0,1:T(8,128)(2,1)} %fusion.46), kind=kOutput, calls=%fused_computation.7.clone.1 | convolution fusion | flops 301989888 | bytes 12730368 | tf_op jit(solution)/shard_map/while/body/eval_jaxpr/bdv,bev->bde/dot_general | solution.py:58
  102.3 0.3 copy.43
  102.7 0.8 copy-done.4
  103.5 1.1 slice_bitcast_fusion.1
  104.6 0.1 copy.23
  104.8 0.1 copy.21
  105.2 0.1 copy.22
  105.3 0.2 multiply_add_fusion
  105.5 0.2 slice.85
  105.6 4.3 %collective-permute-start = (f32[2,64,600]{2,0,1:T(2,128)S(1)}, f32[2,64,600]{2,0,1:T(2,128)S(1)}, u32[]{:S(2)}, u32[]{:S(2)}) collective-permute-start(f32[2,64,600]{2,0,1:T(2,128)S(1)} %slice.85), channel_id=1, source_target_pairs={{0,2},{2,4},{4,6},{6,8},{8,10},{10,12},{12,14},{14,16},{16,18},{18... | collective-permute-start | bytes 921608 | tf_op jit(solution)/shard_map/ppermute | solution.py:12
  110.0 0.1 slice.87
  110.1 1.9 %collective-permute-start.1 = (f32[1,64,600]{2,0,1:T(1,128)S(1)}, f32[1,64,600]{2,0,1:T(1,128)S(1)}, u32[]{:S(2)}, u32[]{:S(2)}) collective-permute-start(f32[1,64,600]{2,0,1:T(1,128)S(1)} %slice.87), channel_id=1, source_target_pairs={{2,0},{4,2},{6,4},{8,6},{10,8},{12,10},{14,12},{16,14},{18,16},{20... | collective-permute-start | bytes 460808 | tf_op jit(solution)/shard_map/ppermute | solution.py:12
  112.1 0.1 reduce_window_sum.11
  112.2 0.2 select_reduce_fusion.1
  112.4 0.1 select_reduce_fusion
  112.5 0.1 fusion.10
  112.6 3.7 %collective-permute-done = f32[2,64,600]{2,0,1:T(2,128)S(1)} collective-permute-done((f32[2,64,600]{2,0,1:T(2,128)S(1)}, f32[2,64,600]{2,0,1:T(2,128)S(1)}, u32[]{:S(2)}, u32[]{:S(2)}) %collective-permute-start) | collective-permute-done | bytes 307232 | tf_op jit(solution)/shard_map/ppermute | solution.py:12
  116.4 0.3 slice_add_fusion
  116.6 5.6 %collective-permute-done.1 = f32[1,64,600]{2,0,1:T(1,128)S(1)} collective-permute-done((f32[1,64,600]{2,0,1:T(1,128)S(1)}, f32[1,64,600]{2,0,1:T(1,128)S(1)}, u32[]{:S(2)}, u32[]{:S(2)}) %collective-permute-start.1) | collective-permute-done | bytes 153632 | tf_op jit(solution)/shard_map/ppermute | solution.py:12
  122.2 0.3 slice_add_fusion.1
  122.5 2.7 %scatter-add.4 = f32[2,64,600]{2,0,1:T(2,128)S(1)} dynamic-update-slice(f32[2,64,600]{2,0,1:T(2,128)S(1)} %slice_add_fusion, f32[1,64,600]{2,0,1:T(1,128)S(1)} %slice_add_fusion.1, s32[]{:T(128)} %constant.202.clone.1, s32[]{:T(128)} %constant.192.clone.1, s32[]{:T(128)} %constant.192.clone.1) | dynamic-update-slice | bytes 307204 | tf_op jit(solution)/shard_map/scatter-add | solution.py:101
  125.2 1.1 gather_fusion
  126.4 0.4 select_bitcast_fusion
  126.7 5.5 %all_to_all.5 = f32[2,96,600]{2,0,1:T(2,128)S(1)} all-to-all(f32[2,96,600]{2,0,1:T(2,128)S(1)} %select_bitcast_fusion), channel_id=1, replica_groups=mesh['tm'=256,'space'=2] {'space'}, dimensions={1} | all-to-all | bytes 921600 | tf_op jit(solution)/shard_map/all_to_all | solution.py:103
  132.3 0.8 copy.24
  133.1 0.2 slice.89
  133.3 0.7 copy.25
  (47 shorter events, 0.7 us)
Async XLA Ops:
  1.3 103.5 %copy-start.7 = (f32[2]{0:T(128)S(1)}, f32[2]{0:T(128)}, u32[]{:S(2)}) copy-start(f32[2]{0:T(128)} %param.15) | copy-start | bytes 28
  1.3 110.8 %copy-start.6 = (s32[64,1]{0,1:T(1,128)S(1)}, s32[64,1]{0,1:T(1,128)}, u32[]{:S(2)}) copy-start(s32[64,1]{0,1:T(1,128)} %param.17) | copy-start | bytes 772
  1.3 1.8 %copy-start.1 = (f32[8,4096]{1,0:T(8,128)}, f32[8,4096]{1,0:T(8,128)S(1)}, u32[]{:S(2)}) copy-start(f32[8,4096]{1,0:T(8,128)S(1)} %get-tuple-element.175) | copy-start | bytes 393220 | tf_op jit(solution)/shard_map/while
  1.3 4.0 %copy-start.5 = (s32[64]{0:T(128)S(1)}, s32[64]{0:T(128)}, u32[]{:S(2)}) copy-start(s32[64]{0:T(128)} %get-tuple-element.178) | copy-start | bytes 772 | tf_op jit(solution)/shard_map/while
  5.5 6.1 %copy-start = (bf16[2,64,4096]{2,1,0:T(8,128)(2,1)S(1)}, bf16[2,64,4096]{2,1,0:T(8,128)(2,1)}, u32[]{:S(2)}) copy-start(bf16[2,64,4096]{2,1,0:T(8,128)(2,1)} %get-tuple-element.177) | copy-start | bytes 3145732 | tf_op jit(solution)/shard_map/while
  25.0 26.5 %copy-start.3 = (f32[2,64,600]{1,2,0:T(8,128)S(1)}, f32[2,64,600]{1,2,0:T(8,128)}, u32[]{:S(2)}) copy-start(f32[2,64,600]{1,2,0:T(8,128)} %get-tuple-element.167) | copy-start | bytes 921604 | tf_op jit(solution)/shard_map/while
  25.0 27.4 %copy-start.2 = (f32[8,4096]{1,0:T(8,128)S(1)}, f32[8,4096]{1,0:T(8,128)}, u32[]{:S(2)}) copy-start(f32[8,4096]{1,0:T(8,128)} %copy-done.1) | copy-start | bytes 393220 | tf_op jit(solution)/shard_map/while
  51.6 0.9 copy-start.4
  52.4 1.8 %copy-start.1 = (f32[8,4096]{1,0:T(8,128)}, f32[8,4096]{1,0:T(8,128)S(1)}, u32[]{:S(2)}) copy-start(f32[8,4096]{1,0:T(8,128)S(1)} %get-tuple-element.175) | copy-start | bytes 393220 | tf_op jit(solution)/shard_map/while
  52.4 4.0 %copy-start.5 = (s32[64]{0:T(128)S(1)}, s32[64]{0:T(128)}, u32[]{:S(2)}) copy-start(s32[64]{0:T(128)} %get-tuple-element.178) | copy-start | bytes 772 | tf_op jit(solution)/shard_map/while
  56.6 6.1 %copy-start = (bf16[2,64,4096]{2,1,0:T(8,128)(2,1)S(1)}, bf16[2,64,4096]{2,1,0:T(8,128)(2,1)}, u32[]{:S(2)}) copy-start(bf16[2,64,4096]{2,1,0:T(8,128)(2,1)} %get-tuple-element.177) | copy-start | bytes 3145732 | tf_op jit(solution)/shard_map/while
  76.1 26.5 %copy-start.3 = (f32[2,64,600]{1,2,0:T(8,128)S(1)}, f32[2,64,600]{1,2,0:T(8,128)}, u32[]{:S(2)}) copy-start(f32[2,64,600]{1,2,0:T(8,128)} %get-tuple-element.167) | copy-start | bytes 921604 | tf_op jit(solution)/shard_map/while
  76.1 27.4 %copy-start.2 = (f32[8,4096]{1,0:T(8,128)S(1)}, f32[8,4096]{1,0:T(8,128)}, u32[]{:S(2)}) copy-start(f32[8,4096]{1,0:T(8,128)} %copy-done.1) | copy-start | bytes 393220 | tf_op jit(solution)/shard_map/while
  102.7 0.9 copy-start.4
  105.6 10.7 %collective-permute-start = (f32[2,64,600]{2,0,1:T(2,128)S(1)}, f32[2,64,600]{2,0,1:T(2,128)S(1)}, u32[]{:S(2)}, u32[]{:S(2)}) collective-permute-start(f32[2,64,600]{2,0,1:T(2,128)S(1)} %slice.85), channel_id=1, source_target_pairs={{0,2},{2,4},{4,6},{6,8},{8,10},{10,12},{12,14},{14,16},{16,18},{18... | collective-permute-start | bytes 921608 | tf_op jit(solution)/shard_map/ppermute | solution.py:12
  110.1 12.1 %collective-permute-start.1 = (f32[1,64,600]{2,0,1:T(1,128)S(1)}, f32[1,64,600]{2,0,1:T(1,128)S(1)}, u32[]{:S(2)}, u32[]{:S(2)}) collective-permute-start(f32[1,64,600]{2,0,1:T(1,128)S(1)} %slice.87), channel_id=1, source_target_pairs={{2,0},{4,2},{6,4},{8,6},{10,8},{12,10},{14,12},{16,14},{18,16},{20... | collective-permute-start | bytes 460808 | tf_op jit(solution)/shard_map/ppermute | solution.py:12
where the time goes:
time: 134 us
  matrix products  79.1 us (59%)
  other arithmetic  18.4 us (14%)
  local copies, waits for them, and re-layouts  14.3 us (11%)
  waiting for transfers between devices  9.33 us (7%)
  starting transfers between devices  6.25 us (5%)
  blocking collectives  5.55 us (4%)
    dot_general x2, matrix products, per_step(): jnp.einsum('bdv,bev->bde', masked, masked, preferred_element_type=jnp.flo...  52.5 us
    dot_general x2, matrix products, per_step(): jnp.einsum('bdv,bv->bd', masked, resid, preferred_element_type=jnp.float32)  26.7 us
    select_n x2, other arithmetic, per_step(): jnp.where(valid_mask[:, None, :], sens, jnp.zeros((), jnp.bfloat16))  12.1 us
    ppermute x2, waiting for transfers between devices, shifted(): return lax.ppermute(block, axis, route)  9.33 us
    ppermute x2, starting transfers between devices, shifted(): return lax.ppermute(block, axis, route)  6.25 us
    all_to_all x1, blocking collectives, per_device(): lax.all_to_all(placed, 'space', split_axis=1, concat_axis=1, tiled=True)  5.55 us
    mul x4, local copies, waits for them, and re-layouts, per_step(): shapes[None, :, None, :] * grads.astype(jnp.float32)[:, None, :, :]  4.25 us
    convert_element_type x2, other arithmetic, per_step(): grads.astype(jnp.float32)[:, None, :, :]  3.61 us
  transfers between devices with their start and end apart: 2, of which 2 were waited for; matrix products, arithmetic and copies ran while one was open for 1% of the time, Pallas kernels for 0%

commit v1 on v0

--- a/solution.py
+++ b/solution.py
@@ -100,7 +100,10 @@
     own_part = own_part.at[:2].add(from_before)
     picked = jnp.take(own_part.at[step_count - 1 :].add(behind), source_brick, axis=1)
     placed = jnp.where(slot_filled[None, :, None], picked, jnp.zeros((), jnp.float32))
-    result = lax.all_to_all(placed, "space", split_axis=1, concat_axis=1, tiled=True)
+    result = jnp.concatenate(
+        lax.all_to_all(jnp.stack(jnp.split(placed, lax.axis_size("space"), axis=1)), "space", 0, 0),
+        axis=1,
+    )
     return (result[:, :, :patch_width], result[:, :, patch_width:])
 
 

time: 134 us -> 134 us (level)
  no operation moved by 1% of the time
where the time goes in v1:
time: 134 us
  matrix products  79.1 us (59%)
  other arithmetic  18.7 us (14%)
  local copies, waits for them, and re-layouts  13.5 us (10%)
  waiting for transfers between devices  9.33 us (7%)
  starting transfers between devices  6.25 us (5%)
  blocking collectives  5.55 us (4%)
    dot_general x2, matrix products, per_step(): jnp.einsum('bdv,bev->bde', masked, masked, preferred_element_type=jnp.flo...  52.5 us
    dot_general x2, matrix products, per_step(): jnp.einsum('bdv,bv->bd', masked, resid, preferred_element_type=jnp.float32)  26.7 us
    select_n x2, other arithmetic, per_step(): jnp.where(valid_mask[:, None, :], sens, jnp.zeros((), jnp.bfloat16))  12.2 us
    ppermute x2, waiting for transfers between devices, shifted(): return lax.ppermute(block, axis, route)  9.33 us
    ppermute x2, starting transfers between devices, shifted(): return lax.ppermute(block, axis, route)  6.25 us
    all_to_all x1, blocking collectives, per_device(): lax.all_to_all(jnp.stack(jnp.split(placed, lax.axis_size('space'), axis=1...  5.55 us
    mul x4, local copies, waits for them, and re-layouts, per_step(): shapes[None, :, None, :] * grads.astype(jnp.float32)[:, None, :, :]  4.24 us
    convert_element_type x2, other arithmetic, per_step(): grads.astype(jnp.float32)[:, None, :, :]  3.61 us
  transfers between devices with their start and end apart: 2, of which 2 were waited for; matrix products, arithmetic and copies ran while one was open for 1% of the time, Pallas kernels for 0%

profile of v1, /device:TPU:255, one launch (start us, length us, event | category | flops | bytes accessed | tf_op | source)
XLA Modules:
  0.0 133.5 jit_solution(3300866078315685001)
XLA Ops:
  0.6 0.1 fusion.30
  0.7 0.1 fusion.24
  0.8 0.1 fusion.28
  0.9 0.1 fusion.22
  1.1 0.2 stack.40
  1.3 102.3 %while.14 = (s32[]{:T(128)}, f32[2,64,600]{1,2,0:T(8,128)}, f32[8,4096]{1,0:T(8,128)S(1)}, bf16[2,64,3,4096]{3,1,2,0:T(8,128)(2,1)}, bf16[2,64,4096]{2,1,0:T(8,128)(2,1)}, /*index=5*/s32[64]{0:T(128)}, s32[]{:T(128)}) while((s32[]{:T(128)}, f32[2,64,600]{1,2,0:T(8,128)}, f32[8,4096]{1,0:T(8,128)S(1)}, ...), condition=%wide.region_6.7_spmd.clone, body=%wide.region_5.6_spmd.clone.sunk | while | flops 334534144 | bytes 58191368 | solution.py:62
  1.3 1.8 %bitcast_convert_fusion.2 = f32[64,3,4096]{2,0,1:T(8,128)S(1)} fusion(bf16[2,64,3,4096]{3,1,2,0:T(8,128)(2,1)} %get-tuple-element.178, s32[]{:T(128)S(6)} %copy.48), kind=kLoop, calls=%fused_computation.9.clone.1 | loop fusion | flops 786432 | bytes 4718596 | tf_op jit(solution)/shard_map/while/body/eval_jaxpr/convert_element_type | solution.py:55
  3.1 0.9 mul.344
  4.0 1.2 mul.345
  5.3 0.2 iota_compare_fusion.6
  5.5 6.1 %fusion.46 = bf16[64,24,4096]{2,0,1:T(8,128)(2,1)} fusion(f32[64,3,4096]{2,0,1:T(8,128)S(1)} %bitcast_convert_fusion.2, f32[24,4096]{1,0:T(8,128)S(1)} %mul.345, pred[64,4096]{1,0:T(8,128)(4,1)S(1)} %iota_compare_fusion.6), kind=kLoop, calls=%fused_computation.4.clone.1 | loop fusion | flops 18874368 | bytes 16384000 | tf_op jit(solution)/shard_map/while/body/eval_jaxpr/jit(_where)/select_n | solution.py:57
  11.6 13.3 %fusion.47 = f32[64,1,24]{2,1,0:T(1,128)S(1)} fusion(bf16[64,24,4096]{2,0,1:T(8,128)(2,1)} %fusion.46, bf16[64,4096,1]{1,0,2:T(8,128)(2,1)S(1)} %dynamic-slice_bitcast_fusion.2), kind=kOutput, calls=%fused_computation.5.clone.1 | convolution fusion | flops 12582912 | bytes 13113344 | tf_op jit(solution)/shard_map/while/body/eval_jaxpr/bdv,bv->bd/dot_general | solution.py:59
  25.0 26.2 %fusion.48 = f32[64,24,24]{2,1,0:T(8,128)S(1)} fusion(bf16[64,24,4096]{2,0,1:T(8,128)(2,1)} %fusion.46), kind=kOutput, calls=%fused_computation.7.clone.1 | convolution fusion | flops 301989888 | bytes 12730368 | tf_op jit(solution)/shard_map/while/body/eval_jaxpr/bdv,bev->bde/dot_general | solution.py:58
  51.3 0.3 copy.44
  51.6 0.8 copy-done.5
  52.4 1.8 %bitcast_convert_fusion.2 = f32[64,3,4096]{2,0,1:T(8,128)S(1)} fusion(bf16[2,64,3,4096]{3,1,2,0:T(8,128)(2,1)} %get-tuple-element.178, s32[]{:T(128)S(6)} %copy.48), kind=kLoop, calls=%fused_computation.9.clone.1 | loop fusion | flops 786432 | bytes 4718596 | tf_op jit(solution)/shard_map/while/body/eval_jaxpr/convert_element_type | solution.py:55
  54.3 0.9 mul.344
  55.2 1.2 mul.345
  56.4 0.2 iota_compare_fusion.6
  56.6 6.1 %fusion.46 = bf16[64,24,4096]{2,0,1:T(8,128)(2,1)} fusion(f32[64,3,4096]{2,0,1:T(8,128)S(1)} %bitcast_convert_fusion.2, f32[24,4096]{1,0:T(8,128)S(1)} %mul.345, pred[64,4096]{1,0:T(8,128)(4,1)S(1)} %iota_compare_fusion.6), kind=kLoop, calls=%fused_computation.4.clone.1 | loop fusion | flops 18874368 | bytes 16384000 | tf_op jit(solution)/shard_map/while/body/eval_jaxpr/jit(_where)/select_n | solution.py:57
  62.8 13.3 %fusion.47 = f32[64,1,24]{2,1,0:T(1,128)S(1)} fusion(bf16[64,24,4096]{2,0,1:T(8,128)(2,1)} %fusion.46, bf16[64,4096,1]{1,0,2:T(8,128)(2,1)S(1)} %dynamic-slice_bitcast_fusion.2), kind=kOutput, calls=%fused_computation.5.clone.1 | convolution fusion | flops 12582912 | bytes 13113344 | tf_op jit(solution)/shard_map/while/body/eval_jaxpr/bdv,bv->bd/dot_general | solution.py:59
  76.2 26.2 %fusion.48 = f32[64,24,24]{2,1,0:T(8,128)S(1)} fusion(bf16[64,24,4096]{2,0,1:T(8,128)(2,1)} %fusion.46), kind=kOutput, calls=%fused_computation.7.clone.1 | convolution fusion | flops 301989888 | bytes 12730368 | tf_op jit(solution)/shard_map/while/body/eval_jaxpr/bdv,bev->bde/dot_general | solution.py:58
  102.4 0.3 copy.44
  102.7 0.8 copy-done.5
  103.6 1.1 slice_bitcast_fusion.1
  104.7 0.1 copy.24
  104.9 0.1 copy.22
  105.0 0.1 select_reduce_fusion.2
  105.2 0.1 copy.23
  105.4 0.2 multiply_add_fusion
  105.5 0.2 slice.85
  105.7 4.3 %collective-permute-start = (f32[2,64,600]{2,0,1:T(2,128)S(1)}, f32[2,64,600]{2,0,1:T(2,128)S(1)}, u32[]{:S(2)}, u32[]{:S(2)}) collective-permute-start(f32[2,64,600]{2,0,1:T(2,128)S(1)} %slice.85), channel_id=1, source_target_pairs={{0,2},{2,4},{4,6},{6,8},{8,10},{10,12},{12,14},{14,16},{16,18},{18... | collective-permute-start | bytes 921608 | tf_op jit(solution)/shard_map/ppermute | solution.py:12
  110.0 0.1 slice.87
  110.2 1.9 %collective-permute-start.1 = (f32[1,64,600]{2,0,1:T(1,128)S(1)}, f32[1,64,600]{2,0,1:T(1,128)S(1)}, u32[]{:S(2)}, u32[]{:S(2)}) collective-permute-start(f32[1,64,600]{2,0,1:T(1,128)S(1)} %slice.87), channel_id=1, source_target_pairs={{2,0},{4,2},{6,4},{8,6},{10,8},{12,10},{14,12},{16,14},{18,16},{20... | collective-permute-start | bytes 460808 | tf_op jit(solution)/shard_map/ppermute | solution.py:12
  112.2 0.1 reduce_window_sum.11
  112.3 0.2 select_reduce_fusion.1
  112.5 0.1 select_reduce_fusion
  112.6 0.1 fusion.10
  112.7 3.7 %collective-permute-done = f32[2,64,600]{2,0,1:T(2,128)S(1)} collective-permute-done((f32[2,64,600]{2,0,1:T(2,128)S(1)}, f32[2,64,600]{2,0,1:T(2,128)S(1)}, u32[]{:S(2)}, u32[]{:S(2)}) %collective-permute-start) | collective-permute-done | bytes 307232 | tf_op jit(solution)/shard_map/ppermute | solution.py:12
  116.4 0.3 slice_add_fusion
  116.7 5.6 %collective-permute-done.1 = f32[1,64,600]{2,0,1:T(1,128)S(1)} collective-permute-done((f32[1,64,600]{2,0,1:T(1,128)S(1)}, f32[1,64,600]{2,0,1:T(1,128)S(1)}, u32[]{:S(2)}, u32[]{:S(2)}) %collective-permute-start.1) | collective-permute-done | bytes 153632 | tf_op jit(solution)/shard_map/ppermute | solution.py:12
  122.3 0.3 slice_add_fusion.1
  122.5 2.7 %scatter-add.4 = f32[2,64,600]{2,0,1:T(2,128)S(1)} dynamic-update-slice(f32[2,64,600]{2,0,1:T(2,128)S(1)} %slice_add_fusion, f32[1,64,600]{2,0,1:T(1,128)S(1)} %slice_add_fusion.1, s32[]{:T(128)} %constant.202.clone.1, s32[]{:T(128)} %constant.192.clone.1, s32[]{:T(128)} %constant.192.clone.1) | dynamic-update-slice | bytes 307204 | tf_op jit(solution)/shard_map/scatter-add | solution.py:101
  125.3 1.1 gather_fusion
  126.4 0.4 select_bitcast_fusion
  126.9 0.2 pad_maximum_fusion
  127.1 5.5 %all_to_all.5 = f32[2,2,48,600]{3,1,2,0:T(2,128)S(1)} all-to-all(f32[2,2,48,600]{3,1,2,0:T(2,128)S(1)} %pad_maximum_fusion), channel_id=1, replica_groups=mesh['tm'=256,'space'=2] {'space'}, dimensions={0} | all-to-all | bytes 921600 | tf_op jit(solution)/shard_map/all_to_all | solution.py:104
  132.8 0.7 copy.26
  (51 shorter events, 0.8 us)
Async XLA Ops:
  1.3 103.6 %copy-start.8 = (f32[2]{0:T(128)S(1)}, f32[2]{0:T(128)}, u32[]{:S(2)}) copy-start(f32[2]{0:T(128)} %param.15) | copy-start | bytes 28
  1.3 110.8 %copy-start.7 = (s32[64,1]{0,1:T(1,128)S(1)}, s32[64,1]{0,1:T(1,128)}, u32[]{:S(2)}) copy-start(s32[64,1]{0,1:T(1,128)} %param.17) | copy-start | bytes 772
  1.3 1.8 %copy-start.1 = (f32[8,4096]{1,0:T(8,128)}, f32[8,4096]{1,0:T(8,128)S(1)}, u32[]{:S(2)}) copy-start(f32[8,4096]{1,0:T(8,128)S(1)} %get-tuple-element.177) | copy-start | bytes 393220 | tf_op jit(solution)/shard_map/while
  1.3 4.0 %copy-start.6 = (s32[64]{0:T(128)S(1)}, s32[64]{0:T(128)}, u32[]{:S(2)}) copy-start(s32[64]{0:T(128)} %get-tuple-element.180) | copy-start | bytes 772 | tf_op jit(solution)/shard_map/while
  5.5 6.1 %copy-start = (bf16[2,64,4096]{2,1,0:T(8,128)(2,1)S(1)}, bf16[2,64,4096]{2,1,0:T(8,128)(2,1)}, u32[]{:S(2)}) copy-start(bf16[2,64,4096]{2,1,0:T(8,128)(2,1)} %get-tuple-element.179) | copy-start | bytes 3145732 | tf_op jit(solution)/shard_map/while
  25.0 26.5 %copy-start.4 = (f32[2,64,600]{1,2,0:T(8,128)S(1)}, f32[2,64,600]{1,2,0:T(8,128)}, u32[]{:S(2)}) copy-start(f32[2,64,600]{1,2,0:T(8,128)} %get-tuple-element.169) | copy-start | bytes 921604 | tf_op jit(solution)/shard_map/while
  25.0 27.4 %copy-start.2 = (f32[8,4096]{1,0:T(8,128)S(1)}, f32[8,4096]{1,0:T(8,128)}, u32[]{:S(2)}) copy-start(f32[8,4096]{1,0:T(8,128)} %copy-done.1) | copy-start | bytes 393220 | tf_op jit(solution)/shard_map/while
  51.6 0.8 copy-start.5
  52.4 1.8 %copy-start.1 = (f32[8,4096]{1,0:T(8,128)}, f32[8,4096]{1,0:T(8,128)S(1)}, u32[]{:S(2)}) copy-start(f32[8,4096]{1,0:T(8,128)S(1)} %get-tuple-element.177) | copy-start | bytes 393220 | tf_op jit(solution)/shard_map/while
  52.4 4.0 %copy-start.6 = (s32[64]{0:T(128)S(1)}, s32[64]{0:T(128)}, u32[]{:S(2)}) copy-start(s32[64]{0:T(128)} %get-tuple-element.180) | copy-start | bytes 772 | tf_op jit(solution)/shard_map/while
  56.6 6.1 %copy-start = (bf16[2,64,4096]{2,1,0:T(8,128)(2,1)S(1)}, bf16[2,64,4096]{2,1,0:T(8,128)(2,1)}, u32[]{:S(2)}) copy-start(bf16[2,64,4096]{2,1,0:T(8,128)(2,1)} %get-tuple-element.179) | copy-start | bytes 3145732 | tf_op jit(solution)/shard_map/while
  76.2 26.5 %copy-start.4 = (f32[2,64,600]{1,2,0:T(8,128)S(1)}, f32[2,64,600]{1,2,0:T(8,128)}, u32[]{:S(2)}) copy-start(f32[2,64,600]{1,2,0:T(8,128)} %get-tuple-element.169) | copy-start | bytes 921604 | tf_op jit(solution)/shard_map/while
  76.2 27.4 %copy-start.2 = (f32[8,4096]{1,0:T(8,128)S(1)}, f32[8,4096]{1,0:T(8,128)}, u32[]{:S(2)}) copy-start(f32[8,4096]{1,0:T(8,128)} %copy-done.1) | copy-start | bytes 393220 | tf_op jit(solution)/shard_map/while
  102.7 0.8 copy-start.5
  105.7 10.7 %collective-permute-start = (f32[2,64,600]{2,0,1:T(2,128)S(1)}, f32[2,64,600]{2,0,1:T(2,128)S(1)}, u32[]{:S(2)}, u32[]{:S(2)}) collective-permute-start(f32[2,64,600]{2,0,1:T(2,128)S(1)} %slice.85), channel_id=1, source_target_pairs={{0,2},{2,4},{4,6},{6,8},{8,10},{10,12},{12,14},{14,16},{16,18},{18... | collective-permute-start | bytes 921608 | tf_op jit(solution)/shard_map/ppermute | solution.py:12
  110.2 12.1 %collective-permute-start.1 = (f32[1,64,600]{2,0,1:T(1,128)S(1)}, f32[1,64,600]{2,0,1:T(1,128)S(1)}, u32[]{:S(2)}, u32[]{:S(2)}) collective-permute-start(f32[1,64,600]{2,0,1:T(1,128)S(1)} %slice.87), channel_id=1, source_target_pairs={{2,0},{4,2},{6,4},{8,6},{10,8},{12,10},{14,12},{16,14},{18,16},{20... | collective-permute-start | bytes 460808 | tf_op jit(solution)/shard_map/ppermute | solution.py:12
  132.7 0.8 copy-start.3
